TPU v7x, 512 devices: a whole 4x8x8 slice. The times are simulated.
512 devices in a mesh: hst: 128 (over z, y, core), local: 4 (over x).
Axes of the slice: x: 4, y: 8, z: 8, core: 2. Of those that a mesh axis runs over, the one named last changes fastest.
Arguments:
- grads: bfloat16 [128, 4, 16, 49152], P('hst', 'local'), may hold values from -1.25 to 1.25
- master: float32 [16, 49152], P('local', 'hst'), may hold values from -3 to 3
- moment_one: float32 [16, 49152], P('local', 'hst'), may hold values from -3 to 3
- moment_two: float32 [16, 49152], P('local', 'hst'), may hold values from 0.01 to 2
Outputs:
- grad_total: float32 [16, 49152], P('local', 'hst')
- new_master: float32 [16, 49152], P('local', 'hst')
- new_one: float32 [16, 49152], P('local', 'hst')
- new_two: float32 [16, 49152], P('local', 'hst')
- secondary: bfloat16 [16, 49152], P('local')
All inputs are finite; a program needn't handle non-finite values.
Results may differ from a plain program's by a relative error of at most 0.001.
Values may be sent and summed in bfloat16 or wider, within the bound.
A program may use at most 64 MiB of HBM per device.

v0:
```python
import jax
import jax.numpy as jnp
from jax import lax
from jax.sharding import PartitionSpec as P

beta_one = 0.9
beta_two = 0.95
learn_rate = 0.02
decay_rate = 0.1
epsilon = 1e-08
correct_one = 1.0 - (0.9**50) ** 2
correct_two = 1.0 - (0.95**50) ** 2


def local(grads, master, moment_one, moment_two):
    local_count = lax.axis_size("local")
    host_count = lax.axis_size("hst")
    gradient = grads[0, 0]
    total_rows = gradient.shape[0]
    total_cols = gradient.shape[1]
    row_block = total_rows // local_count
    col_block = total_cols // host_count
    pieces = lax.all_to_all(
        gradient.reshape(local_count, row_block, total_cols),
        "local",
        split_axis=0,
        concat_axis=0,
        tiled=True,
    )
    partial_sum = jnp.sum(pieces.astype(jnp.float32), axis=0)
    arrived = lax.all_to_all(
        partial_sum.reshape(row_block, host_count, col_block),
        "hst",
        split_axis=1,
        concat_axis=1,
        tiled=True,
    )
    grad_total = jnp.sum(arrived, axis=1)
    new_one = beta_one * moment_one + (1.0 - beta_one) * grad_total
    new_two = beta_two * moment_two + (1.0 - beta_two) * grad_total * grad_total
    update = new_one / correct_one / (jnp.sqrt(new_two / correct_two) + epsilon)
    new_master = master - learn_rate * (update + decay_rate * master)
    secondary = lax.all_gather(new_master.astype(jnp.bfloat16), "hst", axis=1, tiled=True)
    return (grad_total, new_master, new_one, new_two, secondary)


def solution(mesh):
    return jax.shard_map(
        local,
        mesh=mesh,
        in_specs=(
            P("hst", "local", None, None),
            P("local", "hst"),
            P("local", "hst"),
            P("local", "hst"),
        ),
        out_specs=(
            P("local", "hst"),
            P("local", "hst"),
            P("local", "hst"),
            P("local", "hst"),
            P("local", None),
        ),
        check_vma=False,
    )
```

profile of v0, /device:TPU:1, one launch (start us, length us, event | category | flops | bytes accessed | tf_op | source)
XLA Modules:
  0.0 122.6 jit_solution(15280396725466493104)
XLA Ops:
  0.6 1.7 %reshape_squeeze.3 = bf16[4,4,49152]{2,1,0:T(4,128)(2,1)S(1)} reshape(bf16[1,1,16,49152]{3,2,1,0:T(8,128)(2,1)} %param.4) | data formatting | bytes 3145728 | tf_op jit(solution)/shard_map/reshape;squeeze | solution.py:24
  2.4 20.8 %all_to_all.10 = bf16[4,4,49152]{2,1,0:T(4,128)(2,1)S(1)} all-to-all(bf16[4,4,49152]{2,1,0:T(4,128)(2,1)S(1)} %reshape_squeeze.3), channel_id=1, replica_groups=mesh['hst'=128,'local'=4] {'local'}, dimensions={0} | all-to-all | bytes 3145728 | tf_op jit(solution)/shard_map/all_to_all | solution.py:23
  23.2 0.8 convert_reduce_fusion
  24.0 0.0 copy-start.1
  24.0 0.0 copy-start.2
  24.0 0.0 copy-start.3
  24.0 48.3 %all_to_all.11 = f32[4,128,384]{2,0,1:T(4,128)S(1)} all-to-all(f32[4,128,384]{2,0,1:T(4,128)S(1)} %bitcast.3), channel_id=1, replica_groups=mesh['hst'=128,'local'=4] {'hst'}, dimensions={1} | all-to-all | bytes 1572864 | tf_op jit(solution)/shard_map/all_to_all | solution.py:31
  72.3 0.2 reduce_sum.19
  72.5 0.0 copy-done.1
  72.5 0.0 copy-done.2
  72.5 0.0 copy-done.3
  72.5 0.0 copy-start
  72.5 0.6 fusion.1
  73.1 48.7 %all_gather.3 = bf16[4,49152]{1,0:T(4,128)(2,1)S(1)} all-gather(bf16[4,384]{1,0:T(4,128)(2,1)S(1)} %get-tuple-element.5), channel_id=1, replica_groups=mesh['hst'=128,'local'=4] {'hst'}, dimensions={1}, use_global_device_ids=true | all-gather | bytes 396288 | tf_op jit(solution)/shard_map/all_gather | solution.py:43
  121.8 0.7 copy.10
  122.6 0.0 copy-done
Async XLA Ops:
  24.0 48.5 %copy-start.1 = (f32[4,384]{1,0:T(4,128)S(1)}, f32[4,384]{1,0:T(4,128)}, u32[]{:S(2)}) copy-start(f32[4,384]{1,0:T(4,128)} %param.5) | copy-start | bytes 18436
  24.0 48.5 %copy-start.2 = (f32[4,384]{1,0:T(4,128)S(1)}, f32[4,384]{1,0:T(4,128)}, u32[]{:S(2)}) copy-start(f32[4,384]{1,0:T(4,128)} %param.6) | copy-start | bytes 18436
  24.0 48.5 %copy-start.3 = (f32[4,384]{1,0:T(4,128)S(1)}, f32[4,384]{1,0:T(4,128)}, u32[]{:S(2)}) copy-start(f32[4,384]{1,0:T(4,128)} %param.7) | copy-start | bytes 18436
  72.5 50.1 %copy-start = (f32[4,384]{1,0:T(4,128)}, f32[4,384]{1,0:T(4,128)S(1)}, u32[]{:S(2)}) copy-start(f32[4,384]{1,0:T(4,128)S(1)} %reduce_sum.19) | copy-start | bytes 18436
where the time goes:
time: 123 us
  blocking collectives  118 us (96%)
  local copies, waits for them, and re-layouts  2.5 us (2%)
  other arithmetic  1.59 us (1%)
    all_gather x1, blocking collectives, local(): lax.all_gather(new_master.astype(jnp.bfloat16), 'hst', axis=1, tiled=True)  48.7 us
    all_to_all x1, blocking collectives, local(): lax.all_to_all(partial_sum.reshape(row_block, host_count, col_block), 'hs...  48.3 us
    all_to_all x1, blocking collectives, local(): lax.all_to_all(gradient.reshape(local_count, row_block, total_cols), 'loc...  20.8 us

commit v1 on v0

--- a/solution.py
+++ b/solution.py
@@ -40,7 +40,12 @@
     new_two = beta_two * moment_two + (1.0 - beta_two) * grad_total * grad_total
     update = new_one / correct_one / (jnp.sqrt(new_two / correct_two) + epsilon)
     new_master = master - learn_rate * (update + decay_rate * master)
-    secondary = lax.all_gather(new_master.astype(jnp.bfloat16), "hst", axis=1, tiled=True)
+    unit = new_master.astype(jnp.bfloat16)
+    pool = []
+    for _ in range(lax.axis_size("hst")):
+        pool.append(unit)
+    arr_next = lax.all_to_all(jnp.stack(pool), "hst", 0, 0)
+    secondary = jnp.concatenate(arr_next, axis=1)
     return (grad_total, new_master, new_one, new_two, secondary)
 
 

time: 123 us -> 97.5 us (0.79)
  blocking collectives: 118 us -> 92.4 us
    all_gather x1 -> x0, blocking collectives: 48.7 us -> none  [local(): lax.all_gather(new_master.astype(jnp.bfloat16), 'hst', axis=1, tiled=True)]
    all_to_all x0 -> x1, blocking collectives: none -> 23.3 us  [local(): arr_next = lax.all_to_all(jnp.stack(pool), 'hst', 0, 0)]
where the time goes in v1:
time: 97.5 us; the launch traced here: 97.3 us
  blocking collectives  92.4 us (95%)
  local copies, waits for them, and re-layouts  2.6 us (3%)
  other arithmetic  1.59 us (2%)
    all_to_all x1, blocking collectives, local(): lax.all_to_all(partial_sum.reshape(row_block, host_count, col_block), 'hs...  48.3 us
    all_to_all x1, blocking collectives, local(): arr_next = lax.all_to_all(jnp.stack(pool), 'hst', 0, 0)  23.3 us
    all_to_all x1, blocking collectives, local(): lax.all_to_all(gradient.reshape(local_count, row_block, total_cols), 'loc...  20.8 us

profile of v1, /device:TPU:1, one launch (start us, length us, event | category | flops | bytes accessed | tf_op | source)
XLA Modules:
  0.0 97.3 jit_solution(17574983711169281757)
XLA Ops:
  0.6 1.7 %reshape_squeeze.3 = bf16[4,4,49152]{2,1,0:T(4,128)(2,1)S(1)} reshape(bf16[1,1,16,49152]{3,2,1,0:T(8,128)(2,1)} %param.4) | data formatting | bytes 3145728 | tf_op jit(solution)/shard_map/reshape;squeeze | solution.py:24
  2.4 20.8 %all_to_all.15 = bf16[4,4,49152]{2,1,0:T(4,128)(2,1)S(1)} all-to-all(bf16[4,4,49152]{2,1,0:T(4,128)(2,1)S(1)} %reshape_squeeze.3), channel_id=1, replica_groups=mesh['hst'=128,'local'=4] {'local'}, dimensions={0} | all-to-all | bytes 3145728 | tf_op jit(solution)/shard_map/all_to_all | solution.py:23
  23.2 0.8 convert_reduce_fusion
  24.0 0.0 copy-start.1
  24.0 0.0 copy-start.2
  24.0 0.0 copy-start.3
  24.0 48.3 %all_to_all.16 = f32[4,128,384]{2,0,1:T(4,128)S(1)} all-to-all(f32[4,128,384]{2,0,1:T(4,128)S(1)} %bitcast.6), channel_id=1, replica_groups=mesh['hst'=128,'local'=4] {'hst'}, dimensions={1} | all-to-all | bytes 1572864 | tf_op jit(solution)/shard_map/all_to_all | solution.py:31
  72.3 0.2 reduce_sum.19
  72.5 0.0 copy-done.1
  72.5 0.0 copy-done.2
  72.5 0.0 copy-done.3
  72.5 0.0 copy-start
  72.5 0.6 fusion.1
  73.1 0.1 stack.2
  73.2 23.3 %all_to_all.17 = bf16[128,4,384]{2,1,0:T(4,128)(2,1)S(1)} all-to-all(bf16[128,4,384]{2,1,0:T(4,128)(2,1)S(1)} %stack.2), channel_id=1, replica_groups=mesh['hst'=128,'local'=4] {'hst'}, dimensions={0} | all-to-all | bytes 786432 | tf_op jit(solution)/shard_map/all_to_all | solution.py:47
  96.5 0.7 copy.10
  97.3 0.0 copy-done
Async XLA Ops:
  24.0 48.5 %copy-start.1 = (f32[4,384]{1,0:T(4,128)S(1)}, f32[4,384]{1,0:T(4,128)}, u32[]{:S(2)}) copy-start(f32[4,384]{1,0:T(4,128)} %param.5) | copy-start | bytes 18436
  24.0 48.5 %copy-start.2 = (f32[4,384]{1,0:T(4,128)S(1)}, f32[4,384]{1,0:T(4,128)}, u32[]{:S(2)}) copy-start(f32[4,384]{1,0:T(4,128)} %param.6) | copy-start | bytes 18436
  24.0 48.5 %copy-start.3 = (f32[4,384]{1,0:T(4,128)S(1)}, f32[4,384]{1,0:T(4,128)}, u32[]{:S(2)}) copy-start(f32[4,384]{1,0:T(4,128)} %param.7) | copy-start | bytes 18436
  72.5 24.8 %copy-start = (f32[4,384]{1,0:T(4,128)}, f32[4,384]{1,0:T(4,128)S(1)}, u32[]{:S(2)}) copy-start(f32[4,384]{1,0:T(4,128)S(1)} %reduce_sum.19) | copy-start | bytes 18436
